TPU v7x, 128 devices: a whole 4x4x4 slice. The times are simulated.
128 devices in a mesh: dp: 4 (over x), expert: 32 (over z, y, core).
Axes of the slice: x: 4, y: 4, z: 4, core: 2. Of those that a mesh axis runs over, the one named last changes fastest.
Arguments:
- tokens: bfloat16 [16384, 7168], P('expert', 'dp'), may hold values from -6 to 6
- grad_out: bfloat16 [16384, 7168], P('expert', 'dp'), may hold values from -6 to 6
- route_ids: int32 [16384, 1], P('expert'), may hold values from 0 to 31; in each aligned block of 512 rows (0 to 511, 512 to 1023, ...) at most 20 rows name the same one
- gate_codes: int32 [16384, 1], P('expert'), may hold values from 1 to 255
- gate_weight: bfloat16 [32, 7168, 1024], P('expert', 'dp'), may hold values from -0.0625 to 0.0625
- up_weight: bfloat16 [32, 7168, 1024], P('expert', 'dp'), may hold values from -0.0625 to 0.0625
- down_weight: bfloat16 [32, 1024, 7168], P('expert', None, 'dp'), may hold values from -0.1875 to 0.1875
- momentum: bfloat16 [32, 1024, 7168], P('expert', None, 'dp'), may hold values from -6 to 6
Outputs:
- grad_tokens: bfloat16 [16384, 7168], P('expert', 'dp')
- new_down: bfloat16 [32, 1024, 7168], P('expert', None, 'dp')
- new_momentum: bfloat16 [32, 1024, 7168], P('expert', None, 'dp')
Inputs may be any that keep to these rules, and one draw needn't show every extreme that they name: `route_ids`: each token names one expert. Among the 512 tokens of one index of the expert axis no expert is named by more than 20 tokens, a bound that some block reaches.
All inputs are finite; a program needn't handle non-finite values.
Results may differ from a plain program's by a relative error of at most 0.022.
Values may be sent and summed in bfloat16 or wider, within the bound.
A program may use at most 128 MiB of HBM per device.

v0:
```python
import jax
import jax.numpy as jnp
from jax import lax
from jax.sharding import PartitionSpec as P

first_beta = 0.9
second_beta = 0.9
learn_rate = 0.01
decay_rate = 3.0
soft_width = 1.0


def activate(terms):
    pre_gate = terms[:, 0, :]
    pre_up = terms[:, 1, :]
    grad_hidden = terms[:, 2, :]
    sigmoid = jax.nn.sigmoid(pre_gate)
    active = pre_gate * sigmoid
    hidden = (active * pre_up).astype(jnp.bfloat16)
    d_gate = (grad_hidden * pre_up * sigmoid * (1.0 + pre_gate * (1.0 - sigmoid))).astype(
        jnp.bfloat16
    )
    d_up = (grad_hidden * active).astype(jnp.bfloat16)
    return (hidden, d_gate, d_up)


def contract_last(left, right):
    return lax.dot_general(
        left, right, (((1,), (1,)), ((), ())), preferred_element_type=jnp.float32
    )


def contract_first(left, right):
    return lax.dot_general(
        left, right, (((0,), (0,)), ((), ())), preferred_element_type=jnp.float32
    )


def local(tokens, grad_out, route_ids, gate_codes, gate_weight, up_weight, down_weight, momentum):
    n_expert = lax.axis_size("expert")
    tok_rows, slab = tokens.shape
    top = route_ids.shape[1]
    capacity = max(2, tok_rows * top * 5 // (4 * n_expert))
    flat_ids = route_ids.reshape(-1)
    expert_iota = jnp.arange(n_expert, dtype=jnp.int32)
    onehot = (flat_ids[:, None] == expert_iota[None, :]).astype(jnp.int32)
    before = jnp.cumsum(onehot, axis=0) - onehot
    slot = jnp.sum(before * onehot, axis=1)
    target = flat_ids * capacity + slot
    slot_iota = jnp.arange(n_expert * capacity, dtype=jnp.int32)
    placed = (
        (target[None, :] == slot_iota[:, None])
        .astype(jnp.float32)
        .reshape(n_expert * capacity, tok_rows, top)
    )
    route_scale = gate_codes.astype(jnp.float32) / 256.0
    picker = jnp.sum(placed, axis=2).astype(jnp.bfloat16)
    scaler = jnp.sum(placed * route_scale[None, :, :], axis=2).astype(jnp.bfloat16)
    send_x = jnp.dot(picker, tokens, preferred_element_type=jnp.float32).astype(jnp.bfloat16)
    send_dy = jnp.dot(scaler, grad_out, preferred_element_type=jnp.float32).astype(jnp.bfloat16)
    send_x = send_x.reshape(n_expert, capacity, slab)
    send_dy = send_dy.reshape(n_expert, capacity, slab)
    recv_x, recv_dy = (
        lax.all_to_all(send_x, "expert", split_axis=0, concat_axis=0, tiled=True),
        lax.all_to_all(send_dy, "expert", split_axis=0, concat_axis=0, tiled=True),
    )
    x_rows = recv_x.reshape(-1, slab)
    dy_rows = recv_dy.reshape(-1, slab)
    w_gate = gate_weight[0]
    w_up = up_weight[0]
    w_down = down_weight[0]
    dy_part = dy_rows
    gate_part = jnp.dot(x_rows, w_gate, preferred_element_type=jnp.float32)
    up_part = jnp.dot(x_rows, w_up, preferred_element_type=jnp.float32)
    back_part = contract_last(dy_part, w_down)
    shares = lax.psum_scatter(
        jnp.stack([gate_part, up_part, back_part], axis=1).astype(jnp.bfloat16),
        "dp",
        scatter_dimension=0,
        tiled=True,
    ).astype(jnp.float32)
    hidden, d_gate, d_up = activate(shares)
    hidden_part = lax.all_gather(hidden, "dp", axis=0, tiled=True)
    gate_part = lax.all_gather(d_gate, "dp", axis=0, tiled=True)
    up_part = lax.all_gather(d_up, "dp", axis=0, tiled=True)
    dy_part = dy_rows
    grad_w = contract_first(hidden_part, dy_part)
    rows_x = contract_last(gate_part, w_gate) + contract_last(up_part, w_up)
    grad_x = rows_x
    grad_down, grad_x = (grad_w, grad_x)
    back = grad_x.astype(jnp.bfloat16).reshape(n_expert, capacity, slab)
    returned = lax.all_to_all(back, "expert", split_axis=0, concat_axis=0, tiled=True)
    returned = returned.reshape(n_expert * capacity, slab)
    grad_tokens = contract_first(picker, returned).astype(jnp.bfloat16)
    moment = momentum[0].astype(jnp.float32)
    weight = w_down.astype(jnp.float32)
    blend = first_beta * moment + (1.0 - first_beta) * grad_down
    step = blend / jnp.sqrt(blend * blend + soft_width * soft_width)
    agree = jnp.maximum(step * jnp.sign(weight), 0.0)
    new_down = (weight - learn_rate * (step + decay_rate * agree * weight)).astype(jnp.bfloat16)
    new_moment = (second_beta * moment + (1.0 - second_beta) * grad_down).astype(jnp.bfloat16)
    return (grad_tokens, new_down[None], new_moment[None])


def solution(mesh):
    placed = (
        P("expert", "dp"),
        P("expert", "dp"),
        P("expert", None),
        P("expert", None),
        P("expert", "dp", None),
        P("expert", "dp", None),
        P("expert", None, "dp"),
        P("expert", None, "dp"),
    )
    return jax.shard_map(
        local,
        mesh=mesh,
        in_specs=placed,
        out_specs=(P("expert", "dp"), P("expert", None, "dp"), P("expert", None, "dp")),
        check_vma=False,
    )
```

profile of v0, /device:TPU:0, one launch (start us, length us, event | category | flops | bytes accessed | tf_op | source)
XLA Modules:
  0.0 284.5 jit_solution(3125101756731378622)
XLA Ops:
  7.2 0.0 copy-start
  7.2 0.8 fusion.48
  8.0 1.2 reduce-window.6
  9.2 0.2 slice_reduce_fusion
  9.4 0.8 fusion.47
  10.2 0.7 multiply_add_fusion
  10.9 0.0 copy-done
  10.9 2.7 convolution_convert_fusion.1
  13.6 4.1 %reshape.132 = bf16[32,20,1792]{2,1,0:T(8,128)(2,1)} reshape(bf16[640,1792]{1,0:T(8,128)(2,1)} %convolution_convert_fusion.1) | data formatting | bytes 4587520 | tf_op jit(solution)/shard_map/reshape | solution.py:61
  17.7 0.0 copy-start.5
  17.7 8.5 %all-to-all-start = ((bf16[32,20,1792]{2,1,0:T(8,128)(2,1)}), bf16[32,20,1792]{2,1,0:T(8,128)(2,1)S(1)}, u32[]{:S(2)}, u32[]{:S(2)}) async-start(bf16[32,20,1792]{2,1,0:T(8,128)(2,1)} %reshape.132), calls=%async_computation | async-start | bytes 5505024 | tf_op jit(solution)/shard_map/all_to_all | solution.py:64
  26.3 0.0 copy-done.5
  26.3 4.3 %convolution_convert_fusion = bf16[640,1792]{1,0:T(8,128)(2,1)} fusion(bf16[512,1792]{1,0:T(8,128)(2,1)} %param.9, f32[512]{0:T(512)S(1)} %bitcast.104, s32[512]{0:T(512)S(1)} %multiply_add_fusion), kind=kOutput, calls=%fused_computation.24 | convolution fusion | flops 1176207360 | bytes 4132864 | tf_op jit(solution)/shard_map/dot_general | solution.py:60
  30.6 4.1 %reshape.134 = bf16[32,20,1792]{2,1,0:T(8,128)(2,1)} reshape(bf16[640,1792]{1,0:T(8,128)(2,1)} %convolution_convert_fusion) | data formatting | bytes 4587520 | tf_op jit(solution)/shard_map/reshape | solution.py:62
  34.7 29.1 %all-to-all-done = bf16[32,20,1792]{2,1,0:T(8,128)(2,1)S(1)} async-done(((bf16[32,20,1792]{2,1,0:T(8,128)(2,1)}), bf16[32,20,1792]{2,1,0:T(8,128)(2,1)S(1)}, u32[]{:S(2)}, u32[]{:S(2)}) %all-to-all-start) | async-done | bytes 2293792 | tf_op jit(solution)/shard_map/all_to_all | solution.py:64
  63.8 4.8 %all-to-all-start.1 = ((bf16[32,20,1792]{2,1,0:T(8,128)(2,1)}), bf16[32,20,1792]{2,1,0:T(8,128)(2,1)}, u32[]{:S(2)}, u32[]{:S(2)}) async-start(bf16[32,20,1792]{2,1,0:T(8,128)(2,1)} %reshape.134), calls=%async_computation.1 | async-start | bytes 5505024 | tf_op jit(solution)/shard_map/all_to_all | solution.py:65
  68.6 0.0 reduce-scatter.2.cloned.1.call-start
  68.6 2.1 reshape.133
  70.7 0.0 copy-start.2
  70.7 0.0 copy-start.6
  70.7 6.5 %fusion.31 = bf16[640,1,1024]{2,0,1:T(8,128)(2,1)} fusion(bf16[640,1792]{1,0:T(8,128)(2,1)} %reshape.133, bf16[1,1792,1024]{2,1,0:T(8,128)(2,1)} %param.13), kind=kOutput, calls=%fused_computation.31 | convolution fusion | flops 2349465600 | bytes 7274496 | tf_op jit(solution)/shard_map/dot_general | solution.py:74
  77.2 0.0 copy-done.2
  77.2 0.0 copy-done.6
  77.2 3.6 %fusion.34 = bf16[640,1,1024]{2,0,1:T(8,128)(2,1)} fusion(bf16[640,1792]{1,0:T(8,128)(2,1)S(1)} %copy-done.2, bf16[1,1792,1024]{2,1,0:T(8,128)(2,1)S(1)} %copy-done.6), kind=kOutput, calls=%fused_computation.32 | convolution fusion | flops 2349465600 | bytes 7274496 | tf_op jit(solution)/shard_map/dot_general | solution.py:73
  80.8 25.3 %all-to-all-done.1 = bf16[32,20,1792]{2,1,0:T(8,128)(2,1)} async-done(((bf16[32,20,1792]{2,1,0:T(8,128)(2,1)}), bf16[32,20,1792]{2,1,0:T(8,128)(2,1)}, u32[]{:S(2)}, u32[]{:S(2)}) %all-to-all-start.1) | async-done | bytes 2293792 | tf_op jit(solution)/shard_map/all_to_all | solution.py:65
  106.1 2.7 reshape.135
  108.8 0.0 copy-start.3
  108.8 0.0 copy-start.4
  108.8 4.8 %fusion.28 = bf16[640,1,1024]{2,0,1:T(8,128)(2,1)S(1)} fusion(bf16[640,1792]{1,0:T(8,128)(2,1)S(1)} %reshape.135, bf16[1,1024,1792]{2,1,0:T(8,128)(2,1)} %param.14), kind=kOutput, calls=%fused_computation.30 | convolution fusion | flops 2349465600 | bytes 7274496 | tf_op jit(solution)/shard_map/dot_general | solution.py:28
  113.6 0.0 copy-done.3
  113.6 0.0 copy-done.4
  113.6 2.1 pad_maximum_fusion
  115.7 0.0 reduce-scatter.2.cloned.1.call-update
  115.7 0.0 all-gather.6.cloned.1.call-start
  115.8 41.3 %reduce-scatter.2.cloned.1.call-done = bf16[160,3,1024]{2,0,1:T(8,128)(2,1)} async-done(((bf16[640,3,1024]{2,0,1:T(8,128)(2,1)}), bf16[160,3,1024]{2,0,1:T(8,128)(2,1)}) %reduce-scatter.2.cloned.1.call-update) | async-done | bytes 983056 | tf_op jit(solution)/shard_map/reduce_scatter | solution.py:76
  157.1 1.4 convert_element_type.104
  158.5 1.4 multiply_convert_fusion
  159.9 0.0 all-gather.6.cloned.1.call-update
  159.9 0.0 all-gather.4.cloned.1.call-start
  159.9 0.7 all-gather.4.cloned.1.call-update
  160.6 0.2 all-gather.8.cloned.1.call-start
  160.8 0.3 all-gather.8.cloned.1.call-update
  161.2 23.5 %all-gather.6.cloned.1.call-done = bf16[640,1024]{1,0:T(8,128)(2,1)} async-done(((bf16[160,1024]{1,0:T(8,128)(2,1)}), bf16[640,1024]{1,0:T(8,128)(2,1)}) %all-gather.6.cloned.1.call-update) | async-done | bytes 1310736 | tf_op jit(solution)/shard_map/all_gather | solution.py:85
  184.7 7.1 %fusion.8 = f32[640,1792]{1,0:T(8,128)} fusion(bf16[640,1024]{1,0:T(8,128)(2,1)} %all-gather.6.cloned.1.call-done, bf16[1,1792,1024]{2,1,0:T(8,128)(2,1)} %param.13), kind=kOutput, calls=%fused_computation.14 | convolution fusion | flops 2348810240 | bytes 9568256 | tf_op jit(solution)/shard_map/dot_general | solution.py:28
  191.8 20.6 %all-gather.4.cloned.1.call-done = bf16[640,1024]{1,0:T(8,128)(2,1)} async-done(((bf16[160,1024]{1,0:T(8,128)(2,1)}), bf16[640,1024]{1,0:T(8,128)(2,1)}) %all-gather.4.cloned.1.call-update) | async-done | bytes 1310736 | tf_op jit(solution)/shard_map/all_gather | solution.py:84
  212.4 7.8 %add_convert_fusion = bf16[640,1792]{1,0:T(8,128)(2,1)} fusion(f32[640,1792]{1,0:T(8,128)} %fusion.8, bf16[640,1024]{1,0:T(8,128)(2,1)} %all-gather.4.cloned.1.call-done, bf16[1,1792,1024]{2,1,0:T(8,128)(2,1)} %param.12), kind=kOutput, calls=%fused_computation.10 | convolution fusion | flops 2351104000 | bytes 11862016 | tf_op jit(solution)/shard_map/dot_general | solution.py:28
  220.2 4.1 %reshape.136 = bf16[32,20,1792]{2,1,0:T(8,128)(2,1)} reshape(bf16[640,1792]{1,0:T(8,128)(2,1)} %add_convert_fusion) | data formatting | bytes 4587520 | tf_op jit(solution)/shard_map/reshape | solution.py:91
  224.3 7.4 %all-to-all-start.2 = ((bf16[32,20,1792]{2,1,0:T(8,128)(2,1)}), bf16[32,20,1792]{2,1,0:T(8,128)(2,1)}, u32[]{:S(2)}, u32[]{:S(2)}) async-start(bf16[32,20,1792]{2,1,0:T(8,128)(2,1)} %reshape.136), calls=%async_computation.3 | async-start | bytes 5505024 | tf_op jit(solution)/shard_map/all_to_all | solution.py:92
  231.7 8.3 %all-gather.8.cloned.1.call-done = bf16[640,1024]{1,0:T(8,128)(2,1)} async-done(((bf16[160,1024]{1,0:T(8,128)(2,1)}), bf16[640,1024]{1,0:T(8,128)(2,1)}) %all-gather.8.cloned.1.call-update) | async-done | bytes 1310736 | tf_op jit(solution)/shard_map/all_gather | solution.py:83
  240.0 12.7 %convert_bitcast_fusion = (bf16[1,1024,1792]{2,1,0:T(8,128)(2,1)}, bf16[1,1024,1792]{2,1,0:T(8,128)(2,1)}) fusion(bf16[1,1024,1792]{2,1,0:T(8,128)(2,1)} %param.14, bf16[640,1024]{1,0:T(8,128)(2,1)} %all-gather.8.cloned.1.call-done, bf16[640,1792]{1,0:T(8,128)(2,1)S(1)} %reshape.135, bf16[1,1024,1792]{2,1,0:T(8,128)(2,1)} %param.15), kind=kOutput, calls=%fused_computation.22 | convolution fusion | flops 2381840384 | bytes 18284544 | tf_op jit(solution)/shard_map/dot_general | solution.py:34
  252.7 16.5 %all-to-all-done.2 = bf16[32,20,1792]{2,1,0:T(8,128)(2,1)} async-done(((bf16[32,20,1792]{2,1,0:T(8,128)(2,1)}), bf16[32,20,1792]{2,1,0:T(8,128)(2,1)}, u32[]{:S(2)}, u32[]{:S(2)}) %all-to-all-start.2) | async-done | bytes 2293792 | tf_op jit(solution)/shard_map/all_to_all | solution.py:92
  269.1 0.0 copy-start.1
  269.1 4.3 %reshape.137 = bf16[640,1792]{1,0:T(8,128)(2,1)} reshape(bf16[32,20,1792]{2,1,0:T(8,128)(2,1)} %all-to-all-done.2) | data formatting | bytes 4587520 | tf_op jit(solution)/shard_map/reshape | solution.py:93
  273.4 4.5 %convolution_convert_fusion.2 = bf16[512,1792]{1,0:T(8,128)(2,1)} fusion(bf16[640,1792]{1,0:T(8,128)(2,1)} %reshape.137, s32[512]{0:T(512)S(1)} %multiply_add_fusion), kind=kOutput, calls=%fused_computation.26 | convolution fusion | flops 1176305664 | bytes 4130816 | tf_op jit(solution)/shard_map/dot_general | solution.py:34
  277.9 0.0 copy-done.1
  (3 shorter events, 0.0 us)
Async XLA Ops:
  7.2 3.7 %copy-start = (bf16[512,1792]{1,0:T(8,128)(2,1)S(1)}, bf16[512,1792]{1,0:T(8,128)(2,1)}, u32[]{:S(2)}) copy-start(bf16[512,1792]{1,0:T(8,128)(2,1)} %param.8) | copy-start | bytes 5505028
  17.7 8.6 %copy-start.5 = (s32[512,1]{0,1:T(1,128)S(1)}, s32[512,1]{0,1:T(1,128)}, u32[]{:S(2)}) copy-start(s32[512,1]{0,1:T(1,128)} %param.11) | copy-start | bytes 6148
  17.7 46.0 %all-to-all-start = ((bf16[32,20,1792]{2,1,0:T(8,128)(2,1)}), bf16[32,20,1792]{2,1,0:T(8,128)(2,1)S(1)}, u32[]{:S(2)}, u32[]{:S(2)}) async-start(bf16[32,20,1792]{2,1,0:T(8,128)(2,1)} %reshape.132), calls=%async_computation | async-start | bytes 5505024 | tf_op jit(solution)/shard_map/all_to_all | solution.py:64
  63.8 42.3 %all-to-all-start.1 = ((bf16[32,20,1792]{2,1,0:T(8,128)(2,1)}), bf16[32,20,1792]{2,1,0:T(8,128)(2,1)}, u32[]{:S(2)}, u32[]{:S(2)}) async-start(bf16[32,20,1792]{2,1,0:T(8,128)(2,1)} %reshape.134), calls=%async_computation.1 | async-start | bytes 5505024 | tf_op jit(solution)/shard_map/all_to_all | solution.py:65
  68.6 88.5 %reduce-scatter.2.cloned.1.call-start = ((), (), s32[]{:S(2)}) async-start(), calls=%async_computation.4 | async-start | bytes 4915200 | tf_op jit(solution)/shard_map/reduce_scatter | solution.py:76
  70.7 6.5 %copy-start.2 = (bf16[640,1792]{1,0:T(8,128)(2,1)S(1)}, bf16[640,1792]{1,0:T(8,128)(2,1)}, u32[]{:S(2)}) copy-start(bf16[640,1792]{1,0:T(8,128)(2,1)} %reshape.133) | copy-start | bytes 6881284
  70.7 6.5 %copy-start.6 = (bf16[1,1792,1024]{2,1,0:T(8,128)(2,1)S(1)}, bf16[1,1792,1024]{2,1,0:T(8,128)(2,1)}, u32[]{:S(2)}) copy-start(bf16[1,1792,1024]{2,1,0:T(8,128)(2,1)} %param.12) | copy-start | bytes 11010052
  108.8 4.8 %copy-start.3 = (bf16[640,1,1024]{2,0,1:T(8,128)(2,1)S(1)}, bf16[640,1,1024]{2,0,1:T(8,128)(2,1)}, u32[]{:S(2)}) copy-start(bf16[640,1,1024]{2,0,1:T(8,128)(2,1)} %fusion.31) | copy-start | bytes 3932164
  108.8 4.8 %copy-start.4 = (bf16[640,1,1024]{2,0,1:T(8,128)(2,1)S(1)}, bf16[640,1,1024]{2,0,1:T(8,128)(2,1)}, u32[]{:S(2)}) copy-start(bf16[640,1,1024]{2,0,1:T(8,128)(2,1)} %fusion.34) | copy-start | bytes 3932164
  115.7 69.0 %all-gather.6.cloned.1.call-start = ((), (), s32[]{:S(2)}) async-start(), calls=%async_computation.6 | async-start | bytes 1638400 | tf_op jit(solution)/shard_map/all_gather | solution.py:85
  159.9 52.5 %all-gather.4.cloned.1.call-start = ((), (), s32[]{:S(2)}) async-start(), calls=%async_computation.5 | async-start | bytes 1638400 | tf_op jit(solution)/shard_map/all_gather | solution.py:84
  160.6 79.4 %all-gather.8.cloned.1.call-start = ((), (), s32[]{:S(2)}) async-start(), calls=%async_computation.7 | async-start | bytes 1638400 | tf_op jit(solution)/shard_map/all_gather | solution.py:83
  224.3 44.8 %all-to-all-start.2 = ((bf16[32,20,1792]{2,1,0:T(8,128)(2,1)}), bf16[32,20,1792]{2,1,0:T(8,128)(2,1)}, u32[]{:S(2)}, u32[]{:S(2)}) async-start(bf16[32,20,1792]{2,1,0:T(8,128)(2,1)} %reshape.136), calls=%async_computation.3 | async-start | bytes 5505024 | tf_op jit(solution)/shard_map/all_to_all | solution.py:92
  269.1 8.8 %copy-start.1 = (bf16[512,1792]{1,0:T(8,128)(2,1)S(1)}, bf16[512,1792]{1,0:T(8,128)(2,1)}, u32[]{:S(2)}) copy-start(bf16[512,1792]{1,0:T(8,128)(2,1)} %param.8) | copy-start | bytes 5505028
Sparse Core Ops, SparseCore 0:
  115.8 41.1 reduce-scatter.1
  160.0 24.6 all-gather.5
  186.9 25.4 all-gather.3
  214.5 25.4 all-gather.7
where the time goes:
time: 285 us; the launch traced here: 284 us
  waiting for transfers between devices  166 us (58%)
  matrix products  53.9 us (19%)
  local copies, waits for them, and re-layouts  21.6 us (8%)
  starting transfers between devices  21.1 us (7%)
  between operations  13.9 us (5%)
  other arithmetic  8.4 us (3%)
    reduce_scatter x1, waiting for transfers between devices, local(): lax.psum_scatter(jnp.stack([gate_part, up_part, back_part], axis=1).astyp...  41.3 us
    all_to_all x1, waiting for transfers between devices, local(): lax.all_to_all(send_x, 'expert', split_axis=0, concat_axis=0, tiled=True)  29.1 us
    all_to_all x1, waiting for transfers between devices, local(): lax.all_to_all(send_dy, 'expert', split_axis=0, concat_axis=0, tiled=True)  25.3 us
    all_gather x1, waiting for transfers between devices, local(): up_part = lax.all_gather(d_up, 'dp', axis=0, tiled=True)  23.5 us
    all_gather x1, waiting for transfers between devices, local(): gate_part = lax.all_gather(d_gate, 'dp', axis=0, tiled=True)  20.6 us
    dot_general x3, matrix products, contract_last(): lax.dot_general(left, right, (((1,), (1,)), ((), ())), preferred_element_...  19.6 us
    dot_general x2, matrix products, contract_first(): lax.dot_general(left, right, (((0,), (0,)), ((), ())), preferred_element_...  17.2 us
    all_to_all x1, waiting for transfers between devices, local(): lax.all_to_all(back, 'expert', split_axis=0, concat_axis=0, tiled=True)  16.5 us
  transfers between devices with their start and end apart: 7, of which 7 were waited for; matrix products, arithmetic and copies ran while one was open for 18% of the time, Pallas kernels for 0%

commit v1 on v0

--- a/solution.py
+++ b/solution.py
@@ -81,7 +81,23 @@
     ).astype(jnp.float32)
     hidden, d_gate, d_up = activate(shares)
     hidden_part = lax.all_gather(hidden, "dp", axis=0, tiled=True)
-    gate_part = lax.all_gather(d_gate, "dp", axis=0, tiled=True)
+    size, index, rows = (lax.axis_size("dp"), lax.axis_index("dp"), d_gate.shape[0])
+    upward = [(i, (i + 1) % size) for i in range(size)]
+    downward = [(i, (i - 1) % size) for i in range(size)]
+    gate_part = jnp.zeros((*d_gate.shape[:0], size * rows, *d_gate.shape[0 + 1 :]), d_gate.dtype)
+    gate_part = lax.dynamic_update_slice_in_dim(gate_part, d_gate, index * rows, axis=0)
+    from_left = from_right = d_gate
+    half = size // 2
+    for k in range(1, half + 1):
+        from_left = lax.ppermute(from_left, "dp", upward)
+        gate_part = lax.dynamic_update_slice_in_dim(
+            gate_part, from_left, (index - k) % size * rows, axis=0
+        )
+        if k < size - half:
+            from_right = lax.ppermute(from_right, "dp", downward)
+            gate_part = lax.dynamic_update_slice_in_dim(
+                gate_part, from_right, (index + k) % size * rows, axis=0
+            )
     up_part = lax.all_gather(d_up, "dp", axis=0, tiled=True)
     dy_part = dy_rows
     grad_w = contract_first(hidden_part, dy_part)

time: 285 us -> 264 us (0.926)
  waiting for transfers between devices: 166 us -> 147 us
  matrix products: 53.9 us -> 48.8 us
  starting transfers between devices: 21.1 us -> 24.3 us
    ppermute x0 -> x3, waiting for transfers between devices: none -> 25.7 us  [the longest x2 23.9 us: local(): from_left = lax.ppermute(from_left, 'dp', upward)]
    all_gather x1, waiting for transfers between devices: 23.5 us -> 0.93 us  [local(): up_part = lax.all_gather(d_up, 'dp', axis=0, tiled=True)]
    all_gather x1 -> x0, waiting for transfers between devices: 20.6 us -> none  [local(): gate_part = lax.all_gather(d_gate, 'dp', axis=0, tiled=True)]
    dot_general x3, matrix products: 19.6 us -> 14.5 us  [contract_last(): lax.dot_general(left, right, (((1,), (1,)), ((), ())), preferred_element_...]
    ppermute x0 -> x3, starting transfers between devices: none -> 3.24 us  [the longest x1 3 us: local(): from_right = lax.ppermute(from_right, 'dp', downward)]
  transfers between devices with their start and end apart: 7 -> 9, of which waited for: 7 -> 9; matrix products, arithmetic and copies ran while one was open for 18% -> 17% of each run, Pallas kernels for 0% -> 0%
where the time goes in v1:
time: 264 us; the launch traced here: 263 us
  waiting for transfers between devices  147 us (56%)
  matrix products  48.8 us (18%)
  starting transfers between devices  24.3 us (9%)
  local copies, waits for them, and re-layouts  20.1 us (8%)
  between operations  13.9 us (5%)
  other arithmetic  9.16 us (3%)
    reduce_scatter x1, waiting for transfers between devices, local(): lax.psum_scatter(jnp.stack([gate_part, up_part, back_part], axis=1).astyp...  41.3 us
    all_to_all x1, waiting for transfers between devices, local(): lax.all_to_all(send_x, 'expert', split_axis=0, concat_axis=0, tiled=True)  29.1 us
    all_to_all x1, waiting for transfers between devices, local(): lax.all_to_all(send_dy, 'expert', split_axis=0, concat_axis=0, tiled=True)  25.3 us
    ppermute x2, waiting for transfers between devices, local(): from_left = lax.ppermute(from_left, 'dp', upward)  23.9 us
    all_to_all x1, waiting for transfers between devices, local(): lax.all_to_all(back, 'expert', split_axis=0, concat_axis=0, tiled=True)  17.6 us
    dot_general x2, matrix products, contract_first(): lax.dot_general(left, right, (((0,), (0,)), ((), ())), preferred_element_...  17.2 us
    dot_general x3, matrix products, contract_last(): lax.dot_general(left, right, (((1,), (1,)), ((), ())), preferred_element_...  14.5 us
    all_to_all x1, starting transfers between devices, local(): lax.all_to_all(send_x, 'expert', split_axis=0, concat_axis=0, tiled=True)  8.55 us
  transfers between devices with their start and end apart: 9, of which 9 were waited for; matrix products, arithmetic and copies ran while one was open for 17% of the time, Pallas kernels for 0%

profile of v1, /device:TPU:0, one launch (start us, length us, event | category | flops | bytes accessed | tf_op | source)
XLA Modules:
  0.0 263.4 jit_solution(4205187278763887803)
XLA Ops:
  7.2 0.0 copy-start
  7.2 0.8 fusion.48
  8.0 1.2 reduce-window.6
  9.2 0.2 slice_reduce_fusion
  9.4 0.8 fusion.47
  10.2 0.7 multiply_add_fusion
  10.9 0.0 copy-done
  10.9 2.7 %convolution_convert_fusion.1 = bf16[640,1792]{1,0:T(8,128)(2,1)} fusion(bf16[512,1792]{1,0:T(8,128)(2,1)S(1)} %copy-done, s32[512]{0:T(512)S(1)} %multiply_add_fusion), kind=kOutput, calls=%fused_computation.25 | convolution fusion | flops 1176535040 | bytes 4130816 | tf_op jit(solution)/shard_map/dot_general | solution.py:59
  13.6 4.1 %reshape.132 = bf16[32,20,1792]{2,1,0:T(8,128)(2,1)} reshape(bf16[640,1792]{1,0:T(8,128)(2,1)} %convolution_convert_fusion.1) | data formatting | bytes 4587520 | tf_op jit(solution)/shard_map/reshape | solution.py:61
  17.7 0.0 copy-start.8
  17.7 8.5 %all-to-all-start = ((bf16[32,20,1792]{2,1,0:T(8,128)(2,1)}), bf16[32,20,1792]{2,1,0:T(8,128)(2,1)S(1)}, u32[]{:S(2)}, u32[]{:S(2)}) async-start(bf16[32,20,1792]{2,1,0:T(8,128)(2,1)} %reshape.132), calls=%async_computation | async-start | bytes 5505024 | tf_op jit(solution)/shard_map/all_to_all | solution.py:64
  26.3 0.0 copy-done.8
  26.3 4.3 %convolution_convert_fusion = bf16[640,1792]{1,0:T(8,128)(2,1)} fusion(bf16[512,1792]{1,0:T(8,128)(2,1)} %param.9, f32[512]{0:T(512)S(1)} %bitcast.107, s32[512]{0:T(512)S(1)} %multiply_add_fusion), kind=kOutput, calls=%fused_computation.24 | convolution fusion | flops 1176207360 | bytes 4132864 | tf_op jit(solution)/shard_map/dot_general | solution.py:60
  30.6 4.1 %reshape.134 = bf16[32,20,1792]{2,1,0:T(8,128)(2,1)} reshape(bf16[640,1792]{1,0:T(8,128)(2,1)} %convolution_convert_fusion) | data formatting | bytes 4587520 | tf_op jit(solution)/shard_map/reshape | solution.py:62
  34.7 29.1 %all-to-all-done = bf16[32,20,1792]{2,1,0:T(8,128)(2,1)S(1)} async-done(((bf16[32,20,1792]{2,1,0:T(8,128)(2,1)}), bf16[32,20,1792]{2,1,0:T(8,128)(2,1)S(1)}, u32[]{:S(2)}, u32[]{:S(2)}) %all-to-all-start) | async-done | bytes 2293792 | tf_op jit(solution)/shard_map/all_to_all | solution.py:64
  63.8 4.8 %all-to-all-start.1 = ((bf16[32,20,1792]{2,1,0:T(8,128)(2,1)}), bf16[32,20,1792]{2,1,0:T(8,128)(2,1)}, u32[]{:S(2)}, u32[]{:S(2)}) async-start(bf16[32,20,1792]{2,1,0:T(8,128)(2,1)} %reshape.134), calls=%async_computation.1 | async-start | bytes 5505024 | tf_op jit(solution)/shard_map/all_to_all | solution.py:65
  68.6 0.0 reduce-scatter.2.cloned.1.call-start
  68.7 2.1 reshape.133
  70.7 0.0 copy-start.4
  70.7 6.5 %fusion.31 = bf16[640,1,1024]{2,0,1:T(8,128)(2,1)} fusion(bf16[640,1792]{1,0:T(8,128)(2,1)} %reshape.133, bf16[1,1792,1024]{2,1,0:T(8,128)(2,1)} %param.13), kind=kOutput, calls=%fused_computation.31 | convolution fusion | flops 2349465600 | bytes 7274496 | tf_op jit(solution)/shard_map/dot_general | solution.py:74
  77.2 0.0 copy-done.4
  77.2 0.0 copy-done.9
  77.2 3.6 %fusion.34 = bf16[640,1,1024]{2,0,1:T(8,128)(2,1)} fusion(bf16[640,1792]{1,0:T(8,128)(2,1)S(1)} %copy-done.4, bf16[1,1792,1024]{2,1,0:T(8,128)(2,1)S(1)} %copy-done.9), kind=kOutput, calls=%fused_computation.32 | convolution fusion | flops 2349465600 | bytes 7274496 | tf_op jit(solution)/shard_map/dot_general | solution.py:73
  80.8 25.3 %all-to-all-done.1 = bf16[32,20,1792]{2,1,0:T(8,128)(2,1)} async-done(((bf16[32,20,1792]{2,1,0:T(8,128)(2,1)}), bf16[32,20,1792]{2,1,0:T(8,128)(2,1)}, u32[]{:S(2)}, u32[]{:S(2)}) %all-to-all-start.1) | async-done | bytes 2293792 | tf_op jit(solution)/shard_map/all_to_all | solution.py:65
  106.1 2.7 %reshape.135 = bf16[640,1792]{1,0:T(8,128)(2,1)S(1)} reshape(bf16[32,20,1792]{2,1,0:T(8,128)(2,1)} %all-to-all-done.1) | data formatting | bytes 4587520 | tf_op jit(solution)/shard_map/reshape | solution.py:68
  108.8 0.0 copy-start.2
  108.8 0.0 copy-start.6
  108.8 0.0 copy-start.7
  108.8 5.5 %fusion.28 = bf16[640,1,1024]{2,0,1:T(8,128)(2,1)S(1)} fusion(bf16[640,1792]{1,0:T(8,128)(2,1)S(1)} %reshape.135, bf16[1,1024,1792]{2,1,0:T(8,128)(2,1)} %param.14), kind=kOutput, calls=%fused_computation.30 | convolution fusion | flops 2349465600 | bytes 7274496 | tf_op jit(solution)/shard_map/dot_general | solution.py:28
  114.3 0.0 copy-done.2
  114.3 0.0 copy-done.6
  114.3 0.0 copy-done.7
  114.3 2.1 pad_maximum_fusion
  116.4 0.0 reduce-scatter.2.cloned.1.call-update
  116.5 0.0 all-gather.3.cloned.1.call-start
  116.5 41.3 %reduce-scatter.2.cloned.1.call-done = bf16[160,3,1024]{2,0,1:T(8,128)(2,1)} async-done(((bf16[640,3,1024]{2,0,1:T(8,128)(2,1)}), bf16[160,3,1024]{2,0,1:T(8,128)(2,1)}) %reduce-scatter.2.cloned.1.call-update) | async-done | bytes 983056 | tf_op jit(solution)/shard_map/reduce_scatter | solution.py:76
  157.8 1.4 convert_element_type.104
  159.3 1.1 multiply_convert_fusion
  160.3 0.0 all-gather.3.cloned.1.call-update
  160.4 0.0 all-gather.5.cloned.1.call-start
  160.4 0.2 broadcast_in_dim.6
  160.6 1.1 constant_dynamic-update-slice_fusion.3
  161.6 0.2 collective-permute-start
  161.9 3.0 %collective-permute-start.1 = (bf16[160,1024]{1,0:T(8,128)(2,1)}, bf16[160,1024]{1,0:T(8,128)(2,1)S(1)}, u32[]{:S(2)}, u32[]{:S(2)}) collective-permute-start(bf16[160,1024]{1,0:T(8,128)(2,1)} %get-tuple-element.4), channel_id=1, source_target_pairs={{0,96},{32,0},{64,32},{96,64},{1,97},{33,1},{65,33},{97,65},{2,98}... | collective-permute-start | bytes 983048 | tf_op jit(solution)/shard_map/ppermute | solution.py:97
  164.9 7.7 %collective-permute-done = bf16[160,1024]{1,0:T(8,128)(2,1)S(1)} collective-permute-done((bf16[160,1024]{1,0:T(8,128)(2,1)}, bf16[160,1024]{1,0:T(8,128)(2,1)S(1)}, u32[]{:S(2)}, u32[]{:S(2)}) %collective-permute-start) | collective-permute-done | bytes 327712 | tf_op jit(solution)/shard_map/ppermute | solution.py:92
  172.5 0.0 collective-permute-start.2
  172.6 0.0 all-gather.5.cloned.1.call-update
  172.6 1.8 collective-permute-done.1
  174.5 16.2 %collective-permute-done.2 = bf16[160,1024]{1,0:T(8,128)(2,1)S(1)} collective-permute-done((bf16[160,1024]{1,0:T(8,128)(2,1)S(1)}, bf16[160,1024]{1,0:T(8,128)(2,1)S(1)}, u32[]{:S(2)}, u32[]{:S(2)}) %collective-permute-start.2) | collective-permute-done | bytes 327712 | tf_op jit(solution)/shard_map/ppermute | solution.py:92
  190.7 0.0 copy-start.5
  190.7 0.9 all-gather.3.cloned.1.call-done
  191.6 0.1 copy-done.5
  191.7 5.2 %fusion.8 = f32[640,1792]{1,0:T(8,128)S(1)} fusion(bf16[640,1024]{1,0:T(8,128)(2,1)} %all-gather.3.cloned.1.call-done, bf16[1,1792,1024]{2,1,0:T(8,128)(2,1)} %param.13), kind=kOutput, calls=%fused_computation.14 | convolution fusion | flops 2348810240 | bytes 9568256 | tf_op jit(solution)/shard_map/dot_general | solution.py:28
  196.9 0.0 copy-done.10
  196.9 3.9 %add_convert_fusion = bf16[640,1792]{1,0:T(8,128)(2,1)S(1)} fusion(f32[640,1792]{1,0:T(8,128)S(1)} %fusion.8, bf16[640,1024]{1,0:T(8,128)(2,1)} %copy-done.5, bf16[1,1792,1024]{2,1,0:T(8,128)(2,1)S(1)} %copy-done.10), kind=kOutput, calls=%fused_computation.10 | convolution fusion | flops 2351104000 | bytes 11862016 | tf_op jit(solution)/shard_map/dot_general | solution.py:28
  200.8 2.2 reshape.136
  203.1 7.5 %all-to-all-start.2 = ((bf16[32,20,1792]{2,1,0:T(8,128)(2,1)}), bf16[32,20,1792]{2,1,0:T(8,128)(2,1)}, u32[]{:S(2)}, u32[]{:S(2)}) async-start(bf16[32,20,1792]{2,1,0:T(8,128)(2,1)} %reshape.136), calls=%async_computation.3 | async-start | bytes 5505024 | tf_op jit(solution)/shard_map/all_to_all | solution.py:108
  210.6 7.2 %all-gather.5.cloned.1.call-done = bf16[640,1024]{1,0:T(8,128)(2,1)} async-done(((bf16[160,1024]{1,0:T(8,128)(2,1)}), bf16[640,1024]{1,0:T(8,128)(2,1)}) %all-gather.5.cloned.1.call-update) | async-done | bytes 1310736 | tf_op jit(solution)/shard_map/all_gather | solution.py:83
  217.8 0.0 copy-done.3
  217.8 12.7 %convert_bitcast_fusion = (bf16[1,1024,1792]{2,1,0:T(8,128)(2,1)}, bf16[1,1024,1792]{2,1,0:T(8,128)(2,1)}) fusion(bf16[1,1024,1792]{2,1,0:T(8,128)(2,1)} %param.14, bf16[640,1024]{1,0:T(8,128)(2,1)} %all-gather.5.cloned.1.call-done, bf16[640,1792]{1,0:T(8,128)(2,1)S(1)} %copy-done.3, bf16[1,1024,1792]{2,1,0:T(8,128)(2,1)} %param.15), kind=kOutput, calls=%fused_computation.22 | convolution fusion | flops 2381840384 | bytes 18284544 | tf_op jit(solution)/shard_map/dot_general | solution.py:34
  230.5 17.6 %all-to-all-done.2 = bf16[32,20,1792]{2,1,0:T(8,128)(2,1)} async-done(((bf16[32,20,1792]{2,1,0:T(8,128)(2,1)}), bf16[32,20,1792]{2,1,0:T(8,128)(2,1)}, u32[]{:S(2)}, u32[]{:S(2)}) %all-to-all-start.2) | async-done | bytes 2293792 | tf_op jit(solution)/shard_map/all_to_all | solution.py:108
  248.1 4.3 %reshape.137 = bf16[640,1792]{1,0:T(8,128)(2,1)} reshape(bf16[32,20,1792]{2,1,0:T(8,128)(2,1)} %all-to-all-done.2) | data formatting | bytes 4587520 | tf_op jit(solution)/shard_map/reshape | solution.py:109
  252.3 4.5 %convolution_convert_fusion.2 = bf16[512,1792]{1,0:T(8,128)(2,1)} fusion(bf16[640,1792]{1,0:T(8,128)(2,1)} %reshape.137, s32[512]{0:T(512)S(1)} %multiply_add_fusion), kind=kOutput, calls=%fused_computation.26 | convolution fusion | flops 1176305664 | bytes 4130816 | tf_op jit(solution)/shard_map/dot_general | solution.py:34
  256.8 0.0 copy-done.1
  (10 shorter events, 0.1 us)
Async XLA Ops:
  7.2 3.7 %copy-start = (bf16[512,1792]{1,0:T(8,128)(2,1)S(1)}, bf16[512,1792]{1,0:T(8,128)(2,1)}, u32[]{:S(2)}) copy-start(bf16[512,1792]{1,0:T(8,128)(2,1)} %param.8) | copy-start | bytes 5505028
  17.7 8.6 %copy-start.8 = (s32[512,1]{0,1:T(1,128)S(1)}, s32[512,1]{0,1:T(1,128)}, u32[]{:S(2)}) copy-start(s32[512,1]{0,1:T(1,128)} %param.11) | copy-start | bytes 6148
  17.7 46.0 %all-to-all-start = ((bf16[32,20,1792]{2,1,0:T(8,128)(2,1)}), bf16[32,20,1792]{2,1,0:T(8,128)(2,1)S(1)}, u32[]{:S(2)}, u32[]{:S(2)}) async-start(bf16[32,20,1792]{2,1,0:T(8,128)(2,1)} %reshape.132), calls=%async_computation | async-start | bytes 5505024 | tf_op jit(solution)/shard_map/all_to_all | solution.py:64
  63.8 42.3 %all-to-all-start.1 = ((bf16[32,20,1792]{2,1,0:T(8,128)(2,1)}), bf16[32,20,1792]{2,1,0:T(8,128)(2,1)}, u32[]{:S(2)}, u32[]{:S(2)}) async-start(bf16[32,20,1792]{2,1,0:T(8,128)(2,1)} %reshape.134), calls=%async_computation.1 | async-start | bytes 5505024 | tf_op jit(solution)/shard_map/all_to_all | solution.py:65
  68.6 89.2 %reduce-scatter.2.cloned.1.call-start = ((), (), s32[]{:S(2)}) async-start(), calls=%async_computation.4 | async-start | bytes 4915200 | tf_op jit(solution)/shard_map/reduce_scatter | solution.py:76
  70.7 6.5 %copy-start.4 = (bf16[640,1792]{1,0:T(8,128)(2,1)S(1)}, bf16[640,1792]{1,0:T(8,128)(2,1)}, u32[]{:S(2)}) copy-start(bf16[640,1792]{1,0:T(8,128)(2,1)} %reshape.133) | copy-start | bytes 6881284
  70.7 6.5 %copy-start.9 = (bf16[1,1792,1024]{2,1,0:T(8,128)(2,1)S(1)}, bf16[1,1792,1024]{2,1,0:T(8,128)(2,1)}, u32[]{:S(2)}) copy-start(bf16[1,1792,1024]{2,1,0:T(8,128)(2,1)} %param.12) | copy-start | bytes 11010052
  108.8 5.5 %copy-start.2 = (bf16[640,1792]{1,0:T(8,128)(2,1)}, bf16[640,1792]{1,0:T(8,128)(2,1)S(1)}, u32[]{:S(2)}) copy-start(bf16[640,1792]{1,0:T(8,128)(2,1)S(1)} %reshape.135) | copy-start | bytes 6881284
  108.8 5.5 %copy-start.6 = (bf16[640,1,1024]{2,0,1:T(8,128)(2,1)S(1)}, bf16[640,1,1024]{2,0,1:T(8,128)(2,1)}, u32[]{:S(2)}) copy-start(bf16[640,1,1024]{2,0,1:T(8,128)(2,1)} %fusion.31) | copy-start | bytes 3932164
  108.8 5.5 %copy-start.7 = (bf16[640,1,1024]{2,0,1:T(8,128)(2,1)S(1)}, bf16[640,1,1024]{2,0,1:T(8,128)(2,1)}, u32[]{:S(2)}) copy-start(bf16[640,1,1024]{2,0,1:T(8,128)(2,1)} %fusion.34) | copy-start | bytes 3932164
  116.5 75.1 %all-gather.3.cloned.1.call-start = ((), (), s32[]{:S(2)}) async-start(), calls=%async_computation.5 | async-start | bytes 1638400 | tf_op jit(solution)/shard_map/all_gather | solution.py:101
  160.4 57.4 %all-gather.5.cloned.1.call-start = ((), (), s32[]{:S(2)}) async-start(), calls=%async_computation.6 | async-start | bytes 1638400 | tf_op jit(solution)/shard_map/all_gather | solution.py:83
  161.6 10.9 %collective-permute-start = (bf16[160,1024]{1,0:T(8,128)(2,1)}, bf16[160,1024]{1,0:T(8,128)(2,1)S(1)}, u32[]{:S(2)}, u32[]{:S(2)}) collective-permute-start(bf16[160,1024]{1,0:T(8,128)(2,1)} %get-tuple-element.4), channel_id=1, source_target_pairs={{0,32},{32,64},{64,96},{96,0},{1,33},{33,65},{65,97},{97,1},{2,34}... | collective-permute-start | bytes 983048 | tf_op jit(solution)/shard_map/ppermute | solution.py:92
  161.9 12.6 %collective-permute-start.1 = (bf16[160,1024]{1,0:T(8,128)(2,1)}, bf16[160,1024]{1,0:T(8,128)(2,1)S(1)}, u32[]{:S(2)}, u32[]{:S(2)}) collective-permute-start(bf16[160,1024]{1,0:T(8,128)(2,1)} %get-tuple-element.4), channel_id=1, source_target_pairs={{0,96},{32,0},{64,32},{96,64},{1,97},{33,1},{65,33},{97,65},{2,98}... | collective-permute-start | bytes 983048 | tf_op jit(solution)/shard_map/ppermute | solution.py:97
  172.5 18.1 %collective-permute-start.2 = (bf16[160,1024]{1,0:T(8,128)(2,1)S(1)}, bf16[160,1024]{1,0:T(8,128)(2,1)S(1)}, u32[]{:S(2)}, u32[]{:S(2)}) collective-permute-start(bf16[160,1024]{1,0:T(8,128)(2,1)S(1)} %collective-permute-done), channel_id=1, source_target_pairs={{0,32},{32,64},{64,96},{96,0},{1,33},{33,65},{65,97},{97,1},{2,34}... | collective-permute-start | bytes 983048 | tf_op jit(solution)/shard_map/ppermute | solution.py:92
  190.7 1.1 copy-start.5
  191.7 5.2 %copy-start.10 = (bf16[1,1792,1024]{2,1,0:T(8,128)(2,1)S(1)}, bf16[1,1792,1024]{2,1,0:T(8,128)(2,1)}, u32[]{:S(2)}) copy-start(bf16[1,1792,1024]{2,1,0:T(8,128)(2,1)} %param.12) | copy-start | bytes 11010052
  203.1 14.7 %copy-start.3 = (bf16[640,1792]{1,0:T(8,128)(2,1)S(1)}, bf16[640,1792]{1,0:T(8,128)(2,1)}, u32[]{:S(2)}) copy-start(bf16[640,1792]{1,0:T(8,128)(2,1)} %copy-done.2) | copy-start | bytes 6881284
  203.1 45.0 %all-to-all-start.2 = ((bf16[32,20,1792]{2,1,0:T(8,128)(2,1)}), bf16[32,20,1792]{2,1,0:T(8,128)(2,1)}, u32[]{:S(2)}, u32[]{:S(2)}) async-start(bf16[32,20,1792]{2,1,0:T(8,128)(2,1)} %reshape.136), calls=%async_computation.3 | async-start | bytes 5505024 | tf_op jit(solution)/shard_map/all_to_all | solution.py:108
  248.1 8.8 %copy-start.1 = (bf16[512,1792]{1,0:T(8,128)(2,1)S(1)}, bf16[512,1792]{1,0:T(8,128)(2,1)}, u32[]{:S(2)}) copy-start(bf16[512,1792]{1,0:T(8,128)(2,1)} %param.8) | copy-start | bytes 5505028
Sparse Core Ops, SparseCore 0:
  116.6 41.2 reduce-scatter.1
  160.5 31.0 all-gather.2
  193.9 23.9 all-gather.4
